TPU v7x, 512 devices: a whole 4x4x16 slice. The times are simulated.
512 devices in a mesh: kz: 16 (over x, y_hi, core), en: 32 (over y_lo, z).
Axes of the slice: x: 4, y: 4 (y_hi: 2, y_lo: 2; y = y_hi * 2 + y_lo), z: 16, core: 2. Of those that a mesh axis runs over, the one named last changes fastest.
Arguments:
- green: bfloat16 [32, 2, 144, 4096], P('kz', None, None, 'en'), may hold values from -6 to 6
- coupling: bfloat16 [32, 82944], replicated, may hold values from -0.03125 to 0.03125
- kdiff: int32 [32, 32], replicated, may hold values from 0 to 31, each once within a row
- shift: int32 [32], replicated, may hold values from 1 to 8, as said below
- emit_weight: float32 [32], replicated, may hold values from 0.3 to 3
- absorb_weight: float32 [32], replicated, may hold values from 0.3 to 3
- neighbours: int32 [16, 4], replicated, may hold values from 0 to 15
Outputs:
- sigma: float32 [32, 2, 144, 4096], P('kz', None, None, 'en')
Inputs may be any that keep to these rules, and one draw needn't show every extreme that they name: `kdiff`: every row names each momentum point once. `shift`: some entry equals 8.
All inputs are finite; a program needn't handle non-finite values.
Results may differ from a plain program's by a relative error of at most 0.0029.
Values may be sent and summed in bfloat16 or wider, within the bound.
A program may use at most 128 MiB of HBM per device.

v0:
```python
import jax
import jax.numpy as jnp
from jax import lax
from jax.sharding import PartitionSpec as P

HALO = 8


def extended(value, sides, width):
    for axis, dim in sides:
        peers, length = (lax.axis_size(axis), value.shape[dim])
        up = [(i, (i + 1) % peers) for i in range(peers - 1)]
        down = [(j, i) for i, j in up]
        last = lax.slice_in_dim(value, length - width, length, axis=dim)
        first = lax.slice_in_dim(value, 0, width, axis=dim)
        before = lax.ppermute(last, axis, up)
        after = lax.ppermute(first, axis, down)
        value = jnp.concatenate([before, value, after], axis=dim)
    return value


def on_device(green, coupling, kdiff, shift, emit_weight, absorb_weight, neighbours):
    atoms = neighbours.shape[0]
    cols = green.shape[3]
    blocks = green.shape[2]
    local_points = green.shape[0]
    energies = cols // atoms
    margin = HALO * atoms
    whole = lax.all_gather(green, "kz", axis=0, tiled=True)
    widened = extended(whole, (("en", 3),), margin)
    all_points = kdiff.shape[0]
    krows = lax.dynamic_slice_in_dim(kdiff, lax.axis_index("kz") * local_points, local_points, 0)
    couple_all = coupling.reshape(all_points, 4, blocks, blocks)
    phonons = jnp.arange(all_points, dtype=jnp.int32)

    def select_mix(phonon, source_point):
        steps_off = shift[phonon]
        block = lax.dynamic_index_in_dim(widened, source_point, 0, keepdims=False)
        early = lax.dynamic_slice_in_dim(block, (HALO - steps_off) * atoms, cols, 2)
        late = lax.dynamic_slice_in_dim(block, (HALO + steps_off) * atoms, cols, 2)
        mixed = emit_weight[phonon] * early.astype(jnp.float32) + absorb_weight[
            phonon
        ] * late.astype(jnp.float32)
        return mixed.astype(jnp.bfloat16)

    results = []
    for local in range(local_points):
        mixes = jax.vmap(select_mix)(phonons, krows[local])
        projected = jnp.einsum(
            "qjmn,qrnc->jrmc", couple_all, mixes, preferred_element_type=jnp.float32
        )
        projected = projected.reshape(4, 2, blocks, energies, atoms)
        total = jnp.take(projected[0], neighbours[:, 0], axis=3)
        for slot in range(1, 4):
            total = total + jnp.take(projected[slot], neighbours[:, slot], axis=3)
        results.append(total.reshape(2, blocks, cols))
    return jnp.stack(results, 0)


def solution(mesh):
    return jax.shard_map(
        on_device,
        mesh=mesh,
        in_specs=(P("kz", None, None, "en"), P(), P(), P(), P(), P(), P()),
        out_specs=P("kz", None, None, "en"),
        check_vma=False,
    )
```

profile of v0, /device:TPU:8, one launch (start us, length us, event | category | flops | bytes accessed | tf_op | source)
XLA Modules:
  0.0 365.7 jit_solution(10156546521841482820)
XLA Ops:
  6.5 0.7 all-gather.2.cloned.1.call-update
  7.3 71.4 %all-gather.2.cloned.1.call-done = bf16[32,2,144,128]{3,2,1,0:T(8,128)(2,1)} async-done(((bf16[2,2,144,128]{3,2,1,0:T(8,128)(2,1)}), bf16[32,2,144,128]{3,2,1,0:T(8,128)(2,1)}) %all-gather.2.cloned.1.call-update) | async-done | bytes 2359312 | tf_op jit(solution)/shard_map/all_gather | solution.py:29
  78.6 3.5 collective-permute-start
  82.1 5.3 %collective-permute-start.1 = (bf16[32,2,144,128]{3,2,1,0:T(8,128)(2,1)}, bf16[32,2,144,128]{3,2,1,0:T(8,128)(2,1)}, u32[]{:S(2)}, u32[]{:S(2)}) collective-permute-start(bf16[32,2,144,128]{3,2,1,0:T(8,128)(2,1)} %all-gather.2.cloned.1.call-done), channel_id=1, source_target_pairs={{1,0},{2,1},{3,2},{4,3},{5,4},{6,5},{7,6},{8,7},{9,8},{10,9},{11,1... | collective-permute-start | bytes 7077896 | tf_op jit(solution)/shard_map/ppermute | solution.py:17
  87.4 1.4 gather_fusion.2
  88.8 1.4 gather_fusion.3
  90.1 1.4 gather_fusion
  91.5 18.6 %reshape.120 = bf16[32,4,144,144]{3,2,1,0:T(8,128)(2,1)} reshape(bf16[32,82944]{1,0:T(8,128)(2,1)} %param.10) | data formatting | bytes 10616832 | tf_op jit(solution)/shard_map/reshape | solution.py:33
  110.2 27.2 %collective-permute-done = bf16[32,2,144,128]{3,2,1,0:T(8,128)(2,1)} collective-permute-done((bf16[32,2,144,128]{3,2,1,0:T(8,128)(2,1)}, bf16[32,2,144,128]{3,2,1,0:T(8,128)(2,1)}, u32[]{:S(2)}, u32[]{:S(2)}) %collective-permute-start) | collective-permute-done | bytes 2359328 | tf_op jit(solution)/shard_map/ppermute | solution.py:16
  137.4 3.4 constant_dynamic-update-slice_fusion.2
  140.8 1.6 constant_dynamic-update-slice_fusion.1
  142.4 3.4 constant_dynamic-update-slice_fusion
  145.8 7.5 %gather_fusion.1 = bf16[32,2,144,384]{3,2,1,0:T(8,128)(2,1)} fusion(bf16[32,2,144,384]{3,2,1,0:T(8,128)(2,1)} %constant_dynamic-update-slice_fusion, s32[32]{0:T(128)S(1)} %get-tuple-element.32), kind=kCustom, calls=%fused_computation.9 | custom fusion | bytes 14156288 | tf_op jit(solution)/shard_map/vmap(jit(dynamic_index_in_dim))/gather | solution.py:38
  153.3 30.6 %copy.70 = bf16[32,2,144,384]{2,1,0,3:T(2,128)(2,1)} copy(bf16[32,2,144,384]{3,2,1,0:T(8,128)(2,1)} %gather_fusion.1) | data formatting | bytes 14155776 | tf_op jit(solution)/shard_map/vmap(jit(dynamic_index_in_dim))/gather | solution.py:38
  183.9 17.0 %gather_fusion.5 = bf16[32,2,144,128]{2,1,3,0:T(2,128)(2,1)} fusion(bf16[32,2,144,384]{2,1,0,3:T(2,128)(2,1)} %copy.70, s32[32]{0:T(128)S(1)} %get-tuple-element.34), kind=kCustom, calls=%fused_computation.13 | custom fusion | bytes 4719104 | tf_op jit(solution)/shard_map/vmap()/gather | solution.py:39
  200.9 17.0 %gather_fusion.6 = bf16[32,2,144,128]{2,1,3,0:T(2,128)(2,1)} fusion(bf16[32,2,144,384]{2,1,0,3:T(2,128)(2,1)} %copy.70, s32[32]{0:T(128)S(1)} %get-tuple-element.35), kind=kCustom, calls=%fused_computation.14 | custom fusion | bytes 4719104 | tf_op jit(solution)/shard_map/vmap()/gather | solution.py:40
  217.9 7.5 %gather_fusion.4 = bf16[32,2,144,384]{3,2,1,0:T(8,128)(2,1)} fusion(bf16[32,2,144,384]{3,2,1,0:T(8,128)(2,1)} %constant_dynamic-update-slice_fusion, s32[32]{0:T(128)S(1)} %get-tuple-element.33), kind=kCustom, calls=%fused_computation.12 | custom fusion | bytes 14156288 | tf_op jit(solution)/shard_map/vmap(jit(dynamic_index_in_dim))/gather | solution.py:38
  225.3 30.6 %copy.85 = bf16[32,2,144,384]{2,1,0,3:T(2,128)(2,1)} copy(bf16[32,2,144,384]{3,2,1,0:T(8,128)(2,1)} %gather_fusion.4) | data formatting | bytes 14155776 | tf_op jit(solution)/shard_map/vmap(jit(dynamic_index_in_dim))/gather | solution.py:38
  255.9 17.0 %gather_fusion.7 = bf16[32,2,144,128]{2,1,3,0:T(2,128)(2,1)} fusion(bf16[32,2,144,384]{2,1,0,3:T(2,128)(2,1)} %copy.85, s32[32]{0:T(128)S(1)} %get-tuple-element.34), kind=kCustom, calls=%fused_computation.15 | custom fusion | bytes 4719104 | tf_op jit(solution)/shard_map/vmap()/gather | solution.py:39
  272.9 17.0 %gather_fusion.8 = bf16[32,2,144,128]{2,1,3,0:T(2,128)(2,1)} fusion(bf16[32,2,144,384]{2,1,0,3:T(2,128)(2,1)} %copy.85, s32[32]{0:T(128)S(1)} %get-tuple-element.35), kind=kCustom, calls=%fused_computation.16 | custom fusion | bytes 4719104 | tf_op jit(solution)/shard_map/vmap()/gather | solution.py:40
  290.0 9.3 %copy.71 = bf16[32,2,144,128]{3,2,1,0:T(8,128)(2,1)S(1)} copy(bf16[32,2,144,128]{2,1,3,0:T(2,128)(2,1)} %gather_fusion.5) | data formatting | bytes 4718592 | tf_op jit(solution)/shard_map/vmap()/gather | solution.py:39
  299.3 10.6 %copy.73 = bf16[32,2,144,128]{3,2,1,0:T(8,128)(2,1)} copy(bf16[32,2,144,128]{2,1,3,0:T(2,128)(2,1)} %gather_fusion.6) | data formatting | bytes 4718592 | tf_op jit(solution)/shard_map/vmap()/gather | solution.py:40
  309.9 10.7 %copy.86 = bf16[32,2,144,128]{3,2,1,0:T(8,128)(2,1)} copy(bf16[32,2,144,128]{2,1,3,0:T(2,128)(2,1)} %gather_fusion.7) | data formatting | bytes 4718592 | tf_op jit(solution)/shard_map/vmap()/gather | solution.py:39
  320.6 10.6 %copy.88 = bf16[32,2,144,128]{3,2,1,0:T(8,128)(2,1)} copy(bf16[32,2,144,128]{2,1,3,0:T(2,128)(2,1)} %gather_fusion.8) | data formatting | bytes 4718592 | tf_op jit(solution)/shard_map/vmap()/gather | solution.py:40
  331.2 6.6 %fusion.6 = (bf16[32,2,144,128,1]{3,2,1,0,4:T(8,128)(2,1)}, bf16[32,2,144,128,1]{3,2,1,0,4:T(8,128)(2,1)S(1)}) fusion(bf16[32,2,144,128]{3,2,1,0:T(8,128)(2,1)} %copy.73, bf16[32,2,144,128]{3,2,1,0:T(8,128)(2,1)S(1)} %copy.71, f32[32]{0:T(128)S(1)} %gather_fusion.3, f32[32]{0:T(128)S(1)} %gather_fusion, bf16[32,2,144,128]{3,2,1,0:T(8,128)(2,1)} %copy.88, ...), kind=kLoop, calls=%fused_computation.25 | loop fusion | flops 14155776 | bytes 14156032 | tf_op jit(solution)/shard_map/vmap()/convert_element_type | solution.py:44
  337.8 6.0 %fusion.15 = f32[4,2,144,128]{3,2,0,1:T(8,128)S(1)} fusion(bf16[32,4,144,144]{3,2,1,0:T(8,128)(2,1)} %reshape.120, bf16[32,2,144,128,1]{3,2,1,0,4:T(8,128)(2,1)S(1)} %get-tuple-element.31), kind=kOutput, calls=%fused_computation.30 | convolution fusion | flops 1358954496 | bytes 8257536 | tf_op jit(solution)/shard_map/qjmn,qrnc->jrmc/dot_general | solution.py:49
  345.1 6.4 %fusion.10 = f32[4,2,144,128]{3,2,0,1:T(8,128)S(1)} fusion(bf16[32,4,144,144]{3,2,1,0:T(8,128)(2,1)} %reshape.120, bf16[32,2,144,128,1]{3,2,1,0,4:T(8,128)(2,1)} %get-tuple-element.30), kind=kOutput, calls=%fused_computation.29 | convolution fusion | flops 1358954496 | bytes 8257536 | tf_op jit(solution)/shard_map/qjmn,qrnc->jrmc/dot_general | solution.py:49
  351.8 0.6 gather_fusion.13
  352.4 0.6 gather_fusion.9
  353.3 0.6 gather_fusion.14
  353.8 0.6 gather_fusion.10
  357.9 0.9 copy.100
  (44 shorter events, 5.3 us)
Async XLA Ops:
  6.5 103.5 %copy-start = (s32[32,32]{1,0:T(8,128)S(1)}, s32[32,32]{1,0:T(8,128)}, u32[]{:S(2)}) copy-start(s32[32,32]{1,0:T(8,128)} %param.11) | copy-start | bytes 12292
  6.5 72.1 %all-gather.2.cloned.1.call-start = ((), (), s32[]{:S(2)}) async-start(), calls=%async_computation | async-start | bytes 2506752 | tf_op jit(solution)/shard_map/all_gather | solution.py:29
  78.6 58.8 %collective-permute-start = (bf16[32,2,144,128]{3,2,1,0:T(8,128)(2,1)}, bf16[32,2,144,128]{3,2,1,0:T(8,128)(2,1)}, u32[]{:S(2)}, u32[]{:S(2)}) collective-permute-start(bf16[32,2,144,128]{3,2,1,0:T(8,128)(2,1)} %all-gather.2.cloned.1.call-done), channel_id=1, source_target_pairs={{0,1},{1,2},{2,3},{3,4},{4,5},{5,6},{6,7},{7,8},{8,9},{9,10},{10,1... | collective-permute-start | bytes 7077896 | tf_op jit(solution)/shard_map/ppermute | solution.py:16
  82.1 60.3 %collective-permute-start.1 = (bf16[32,2,144,128]{3,2,1,0:T(8,128)(2,1)}, bf16[32,2,144,128]{3,2,1,0:T(8,128)(2,1)}, u32[]{:S(2)}, u32[]{:S(2)}) collective-permute-start(bf16[32,2,144,128]{3,2,1,0:T(8,128)(2,1)} %all-gather.2.cloned.1.call-done), channel_id=1, source_target_pairs={{1,0},{2,1},{3,2},{4,3},{5,4},{6,5},{7,6},{8,7},{9,8},{10,9},{11,1... | collective-permute-start | bytes 7077896 | tf_op jit(solution)/shard_map/ppermute | solution.py:17
  91.5 18.6 %copy-start.3 = (s32[16,4]{0,1:T(4,128)S(1)}, s32[16,4]{0,1:T(4,128)}, u32[]{:S(2)}) copy-start(s32[16,4]{0,1:T(4,128)} %param.15) | copy-start | bytes 772
  110.1 30.7 %copy-start.2 = (bf16[32,2,144,128]{3,2,1,0:T(8,128)(2,1)S(1)}, bf16[32,2,144,128]{3,2,1,0:T(8,128)(2,1)}, u32[]{:S(2)}) copy-start(bf16[32,2,144,128]{3,2,1,0:T(8,128)(2,1)} %all-gather.2.cloned.1.call-done) | copy-start | bytes 7077892
  356.1 2.7 copy-start.1
Sparse Core Ops, SparseCore 0:
  10.6 67.9 all-gather.1
where the time goes:
time: 369 us; the launch traced here: 366 us
  local copies, waits for them, and re-layouts  225 us (61%)
  waiting for transfers between devices  99.3 us (27%)
  between operations  13.7 us (4%)
  matrix products  12.4 us (3%)
  starting transfers between devices  8.74 us (2%)
  other arithmetic  6.9 us (2%)
    gather x4, local copies, waits for them, and re-layouts, select_mix(): block = lax.dynamic_index_in_dim(widened, source_point, 0, keepdims=False)  76.1 us
    all_gather x1, waiting for transfers between devices, on_device(): whole = lax.all_gather(green, 'kz', axis=0, tiled=True)  71.4 us
    gather x4, local copies, waits for them, and re-layouts, select_mix(): late = lax.dynamic_slice_in_dim(block, (HALO + steps_off) * atoms, cols, 2)  55.3 us
    gather x4, local copies, waits for them, and re-layouts, select_mix(): early = lax.dynamic_slice_in_dim(block, (HALO - steps_off) * atoms, cols, 2)  53.9 us
    ppermute x1, waiting for transfers between devices, extended(): before = lax.ppermute(last, axis, up)  27.2 us
    reshape x1, local copies, waits for them, and re-layouts, on_device(): couple_all = coupling.reshape(all_points, 4, blocks, blocks)  18.6 us
    dot_general x2, matrix products, on_device(): jnp.einsum('qjmn,qrnc->jrmc', couple_all, mixes, preferred_element_type=j...  12.4 us
  transfers between devices with their start and end apart: 3, of which 2 were waited for; matrix products, arithmetic and copies ran while one was open for 8% of the time, Pallas kernels for 0%

commit v1 on v0

--- a/solution.py
+++ b/solution.py
@@ -4,6 +4,9 @@
 from jax.sharding import PartitionSpec as P
 
 HALO = 8
+load_steps_all_now = lambda point, axis_key: jnp.concatenate(
+    lax.all_to_all(jnp.stack(lax.axis_size(axis_key) * [point], 0), axis_key, 0, 0), 0
+)
 
 
 def extended(value, sides, width):
@@ -26,7 +29,7 @@
     local_points = green.shape[0]
     energies = cols // atoms
     margin = HALO * atoms
-    whole = lax.all_gather(green, "kz", axis=0, tiled=True)
+    whole = load_steps_all_now(green, "kz")
     widened = extended(whole, (("en", 3),), margin)
     all_points = kdiff.shape[0]
     krows = lax.dynamic_slice_in_dim(kdiff, lax.axis_index("kz") * local_points, local_points, 0)

time: 369 us -> 326 us (0.88)
  waiting for transfers between devices: 99.3 us -> 29.9 us
  blocking collectives: 0 us -> 37.6 us
  between operations: 13.7 us -> 0.38 us
  local copies, waits for them, and re-layouts: 225 us -> 216 us
  other arithmetic: 6.9 us -> 12.8 us
  starting transfers between devices: 8.74 us -> 14.1 us
    all_gather x1 -> x0, waiting for transfers between devices: 71.4 us -> none  [on_device(): whole = lax.all_gather(green, 'kz', axis=0, tiled=True)]
    all_to_all x0 -> x1, blocking collectives: none -> 37.6 us  [lax.all_to_all(jnp.stack(lax.axis_size(axis_key) * [point], 0), axis_key,...]
    concatenate x0 -> x1, other arithmetic: none -> 5.89 us  [extended(): value = jnp.concatenate([before, value, after], axis=dim)]
    ppermute x1, starting transfers between devices: 5.29 us -> 10.3 us  [extended(): after = lax.ppermute(first, axis, down)]
    unnamed x10 -> x12, local copies, waits for them, and re-layouts: 5.01 us -> 0.03 us
  transfers between devices with their start and end apart: 3 -> 2, of which waited for: 2 -> 2; matrix products, arithmetic and copies ran while one was open for 8% -> 6% of each run, Pallas kernels for 0% -> 0%
where the time goes in v1:
time: 326 us; the launch traced here: 323 us
  local copies, waits for them, and re-layouts  216 us (66%)
  blocking collectives  37.6 us (12%)
  waiting for transfers between devices  29.9 us (9%)
  starting transfers between devices  14.1 us (4%)
  other arithmetic  12.8 us (4%)
  matrix products  12.4 us (4%)
    gather x4, local copies, waits for them, and re-layouts, select_mix(): block = lax.dynamic_index_in_dim(widened, source_point, 0, keepdims=False)  76.1 us
    gather x4, local copies, waits for them, and re-layouts, select_mix(): late = lax.dynamic_slice_in_dim(block, (HALO + steps_off) * atoms, cols, 2)  55.3 us
    gather x4, local copies, waits for them, and re-layouts, select_mix(): early = lax.dynamic_slice_in_dim(block, (HALO - steps_off) * atoms, cols, 2)  54.1 us
    all_to_all x1, blocking collectives, lax.all_to_all(jnp.stack(lax.axis_size(axis_key) * [point], 0), axis_key,...  37.6 us
    ppermute x1, waiting for transfers between devices, extended(): before = lax.ppermute(last, axis, up)  28.8 us
    reshape x1, local copies, waits for them, and re-layouts, on_device(): couple_all = coupling.reshape(all_points, 4, blocks, blocks)  18.6 us
    dot_general x2, matrix products, on_device(): jnp.einsum('qjmn,qrnc->jrmc', couple_all, mixes, preferred_element_type=j...  12.4 us
    ppermute x1, starting transfers between devices, extended(): after = lax.ppermute(first, axis, down)  10.3 us
  transfers between devices with their start and end apart: 2, of which 2 were waited for; matrix products, arithmetic and copies ran while one was open for 6% of the time, Pallas kernels for 0%

profile of v1, /device:TPU:8, one launch (start us, length us, event | category | flops | bytes accessed | tf_op | source)
XLA Modules:
  0.0 322.9 jit_solution(13322411211470467201)
XLA Ops:
  0.0 1.4 stack.4
  1.4 37.6 %all_to_all.5 = bf16[16,2,2,144,128]{4,3,2,1,0:T(8,128)(2,1)S(1)} all-to-all(bf16[16,2,2,144,128]{4,3,2,1,0:T(8,128)(2,1)S(1)} %stack.4), channel_id=1, replica_groups=mesh['kz'=16,'en'=32] {'kz'}, dimensions={0} | all-to-all | bytes 4718592 | tf_op jit(solution)/shard_map/all_to_all | solution.py:8
  39.0 3.8 %collective-permute-start = (bf16[32,2,144,128]{3,2,1,0:T(8,128)(2,1)S(1)}, bf16[32,2,144,128]{3,2,1,0:T(8,128)(2,1)}, u32[]{:S(2)}, u32[]{:S(2)}) collective-permute-start(bf16[32,2,144,128]{3,2,1,0:T(8,128)(2,1)S(1)} %bitcast.91), channel_id=1, source_target_pairs={{0,1},{1,2},{2,3},{3,4},{4,5},{5,6},{6,7},{7,8},{8,9},{9,10},{10,1... | collective-permute-start | bytes 7077896 | tf_op jit(solution)/shard_map/ppermute | solution.py:19
  42.8 10.3 %collective-permute-start.1 = (bf16[32,2,144,128]{3,2,1,0:T(8,128)(2,1)S(1)}, bf16[32,2,144,128]{3,2,1,0:T(8,128)(2,1)}, u32[]{:S(2)}, u32[]{:S(2)}) collective-permute-start(bf16[32,2,144,128]{3,2,1,0:T(8,128)(2,1)S(1)} %bitcast.92), channel_id=1, source_target_pairs={{1,0},{2,1},{3,2},{4,3},{5,4},{6,5},{7,6},{8,7},{9,8},{10,9},{11,1... | collective-permute-start | bytes 7077896 | tf_op jit(solution)/shard_map/ppermute | solution.py:20
  53.2 0.7 gather_fusion.2
  53.9 0.7 gather_fusion.3
  54.6 0.7 gather_fusion
  55.3 18.6 %reshape.126 = bf16[32,4,144,144]{3,2,1,0:T(8,128)(2,1)} reshape(bf16[32,82944]{1,0:T(8,128)(2,1)} %param.10) | data formatting | bytes 10616832 | tf_op jit(solution)/shard_map/reshape | solution.py:36
  74.0 28.8 %collective-permute-done = bf16[32,2,144,128]{3,2,1,0:T(8,128)(2,1)} collective-permute-done((bf16[32,2,144,128]{3,2,1,0:T(8,128)(2,1)S(1)}, bf16[32,2,144,128]{3,2,1,0:T(8,128)(2,1)}, u32[]{:S(2)}, u32[]{:S(2)}) %collective-permute-start) | collective-permute-done | bytes 2359328 | tf_op jit(solution)/shard_map/ppermute | solution.py:19
  102.8 1.1 collective-permute-done.1
  103.9 5.9 %pad_maximum_fusion = bf16[32,2,144,384]{3,2,1,0:T(8,128)(2,1)} fusion(bf16[32,2,144,128]{3,2,1,0:T(8,128)(2,1)} %collective-permute-done.1, bf16[32,2,144,128]{3,2,1,0:T(8,128)(2,1)S(1)} %bitcast.93, bf16[32,2,144,128]{3,2,1,0:T(8,128)(2,1)} %collective-permute-done), kind=kLoop, calls=%fused_computation.23 | loop fusion | flops 21233664 | bytes 14155776 | tf_op jit(solution)/shard_map/concatenate | solution.py:21
  109.8 7.5 %gather_fusion.1 = bf16[32,2,144,384]{3,2,1,0:T(8,128)(2,1)} fusion(bf16[32,2,144,384]{3,2,1,0:T(8,128)(2,1)} %pad_maximum_fusion, s32[32]{0:T(128)S(1)} %get-tuple-element.32), kind=kCustom, calls=%fused_computation.9 | custom fusion | bytes 14156288 | tf_op jit(solution)/shard_map/vmap(jit(dynamic_index_in_dim))/gather | solution.py:41
  117.2 30.6 %copy.43 = bf16[32,2,144,384]{2,1,0,3:T(2,128)(2,1)} copy(bf16[32,2,144,384]{3,2,1,0:T(8,128)(2,1)} %gather_fusion.1) | data formatting | bytes 14155776 | tf_op jit(solution)/shard_map/vmap(jit(dynamic_index_in_dim))/gather | solution.py:41
  147.8 16.9 %gather_fusion.5 = bf16[32,2,144,128]{2,1,3,0:T(2,128)(2,1)} fusion(bf16[32,2,144,384]{2,1,0,3:T(2,128)(2,1)} %copy.43, s32[32]{0:T(128)S(1)} %get-tuple-element.34), kind=kCustom, calls=%fused_computation.13 | custom fusion | bytes 4719104 | tf_op jit(solution)/shard_map/vmap()/gather | solution.py:42
  164.8 17.0 %gather_fusion.6 = bf16[32,2,144,128]{2,1,3,0:T(2,128)(2,1)} fusion(bf16[32,2,144,384]{2,1,0,3:T(2,128)(2,1)} %copy.43, s32[32]{0:T(128)S(1)} %get-tuple-element.35), kind=kCustom, calls=%fused_computation.14 | custom fusion | bytes 4719104 | tf_op jit(solution)/shard_map/vmap()/gather | solution.py:43
  181.8 7.5 %gather_fusion.4 = bf16[32,2,144,384]{3,2,1,0:T(8,128)(2,1)} fusion(bf16[32,2,144,384]{3,2,1,0:T(8,128)(2,1)} %pad_maximum_fusion, s32[32]{0:T(128)S(1)} %get-tuple-element.33), kind=kCustom, calls=%fused_computation.12 | custom fusion | bytes 14156288 | tf_op jit(solution)/shard_map/vmap(jit(dynamic_index_in_dim))/gather | solution.py:41
  189.2 30.6 %copy.58 = bf16[32,2,144,384]{2,1,0,3:T(2,128)(2,1)} copy(bf16[32,2,144,384]{3,2,1,0:T(8,128)(2,1)} %gather_fusion.4) | data formatting | bytes 14155776 | tf_op jit(solution)/shard_map/vmap(jit(dynamic_index_in_dim))/gather | solution.py:41
  219.8 17.2 %gather_fusion.7 = bf16[32,2,144,128]{2,1,3,0:T(2,128)(2,1)} fusion(bf16[32,2,144,384]{2,1,0,3:T(2,128)(2,1)} %copy.58, s32[32]{0:T(128)S(1)} %get-tuple-element.34), kind=kCustom, calls=%fused_computation.15 | custom fusion | bytes 4719104 | tf_op jit(solution)/shard_map/vmap()/gather | solution.py:42
  237.0 17.0 %gather_fusion.8 = bf16[32,2,144,128]{2,1,3,0:T(2,128)(2,1)} fusion(bf16[32,2,144,384]{2,1,0,3:T(2,128)(2,1)} %copy.58, s32[32]{0:T(128)S(1)} %get-tuple-element.35), kind=kCustom, calls=%fused_computation.16 | custom fusion | bytes 4719104 | tf_op jit(solution)/shard_map/vmap()/gather | solution.py:43
  254.1 9.3 %copy.44 = bf16[32,2,144,128]{3,2,1,0:T(8,128)(2,1)S(1)} copy(bf16[32,2,144,128]{2,1,3,0:T(2,128)(2,1)} %gather_fusion.5) | data formatting | bytes 4718592 | tf_op jit(solution)/shard_map/vmap()/gather | solution.py:42
  263.4 10.6 %copy.46 = bf16[32,2,144,128]{3,2,1,0:T(8,128)(2,1)} copy(bf16[32,2,144,128]{2,1,3,0:T(2,128)(2,1)} %gather_fusion.6) | data formatting | bytes 4718592 | tf_op jit(solution)/shard_map/vmap()/gather | solution.py:43
  274.0 10.7 %copy.59 = bf16[32,2,144,128]{3,2,1,0:T(8,128)(2,1)} copy(bf16[32,2,144,128]{2,1,3,0:T(2,128)(2,1)} %gather_fusion.7) | data formatting | bytes 4718592 | tf_op jit(solution)/shard_map/vmap()/gather | solution.py:42
  284.7 10.6 %copy.61 = bf16[32,2,144,128]{3,2,1,0:T(8,128)(2,1)} copy(bf16[32,2,144,128]{2,1,3,0:T(2,128)(2,1)} %gather_fusion.8) | data formatting | bytes 4718592 | tf_op jit(solution)/shard_map/vmap()/gather | solution.py:43
  295.3 6.6 %fusion.6 = (bf16[32,2,144,128,1]{3,2,1,0,4:T(8,128)(2,1)}, bf16[32,2,144,128,1]{3,2,1,0,4:T(8,128)(2,1)S(1)}) fusion(bf16[32,2,144,128]{3,2,1,0:T(8,128)(2,1)} %copy.46, bf16[32,2,144,128]{3,2,1,0:T(8,128)(2,1)S(1)} %copy.44, f32[32]{0:T(128)S(1)} %gather_fusion.3, f32[32]{0:T(128)S(1)} %gather_fusion, bf16[32,2,144,128]{3,2,1,0:T(8,128)(2,1)} %copy.61, ...), kind=kLoop, calls=%fused_computation.26 | loop fusion | flops 14155776 | bytes 14156032 | tf_op jit(solution)/shard_map/vmap()/convert_element_type | solution.py:47
  301.9 5.8 %fusion.15 = f32[4,2,144,128]{3,2,0,1:T(8,128)S(1)} fusion(bf16[32,4,144,144]{3,2,1,0:T(8,128)(2,1)} %reshape.126, bf16[32,2,144,128,1]{3,2,1,0,4:T(8,128)(2,1)S(1)} %get-tuple-element.31), kind=kOutput, calls=%fused_computation.31 | convolution fusion | flops 1358954496 | bytes 8257536 | tf_op jit(solution)/shard_map/qjmn,qrnc->jrmc/dot_general | solution.py:52
  308.9 6.6 %fusion.10 = f32[4,2,144,128]{3,2,0,1:T(8,128)S(1)} fusion(bf16[32,4,144,144]{3,2,1,0:T(8,128)(2,1)} %reshape.126, bf16[32,2,144,128,1]{3,2,1,0,4:T(8,128)(2,1)} %get-tuple-element.30), kind=kOutput, calls=%fused_computation.30 | convolution fusion | flops 1358954496 | bytes 8257536 | tf_op jit(solution)/shard_map/qjmn,qrnc->jrmc/dot_general | solution.py:52
  315.9 0.6 gather_fusion.13
  316.5 0.6 gather_fusion.9
  317.3 0.6 gather_fusion.14
  318.8 0.6 gather_fusion.15
  319.4 0.6 gather_fusion.11
  322.0 0.9 copy.73
  (45 shorter events, 4.7 us)
Async XLA Ops:
  0.0 73.9 %copy-start = (s32[32,32]{1,0:T(8,128)S(1)}, s32[32,32]{1,0:T(8,128)}, u32[]{:S(2)}) copy-start(s32[32,32]{1,0:T(8,128)} %param.11) | copy-start | bytes 12292
  0.0 53.1 %copy-start.2 = (s32[32]{0:T(128)S(1)}, s32[32]{0:T(128)}, u32[]{:S(2)}) copy-start(s32[32]{0:T(128)} %param.12) | copy-start | bytes 388
  0.0 53.9 %copy-start.3 = (f32[32]{0:T(128)S(1)}, f32[32]{0:T(128)}, u32[]{:S(2)}) copy-start(f32[32]{0:T(128)} %param.14) | copy-start | bytes 388
  0.0 54.6 %copy-start.4 = (f32[32]{0:T(128)S(1)}, f32[32]{0:T(128)}, u32[]{:S(2)}) copy-start(f32[32]{0:T(128)} %param.13) | copy-start | bytes 388
  39.0 63.8 %collective-permute-start = (bf16[32,2,144,128]{3,2,1,0:T(8,128)(2,1)S(1)}, bf16[32,2,144,128]{3,2,1,0:T(8,128)(2,1)}, u32[]{:S(2)}, u32[]{:S(2)}) collective-permute-start(bf16[32,2,144,128]{3,2,1,0:T(8,128)(2,1)S(1)} %bitcast.91), channel_id=1, source_target_pairs={{0,1},{1,2},{2,3},{3,4},{4,5},{5,6},{6,7},{7,8},{8,9},{9,10},{10,1... | collective-permute-start | bytes 7077896 | tf_op jit(solution)/shard_map/ppermute | solution.py:19
  42.8 61.1 %collective-permute-start.1 = (bf16[32,2,144,128]{3,2,1,0:T(8,128)(2,1)S(1)}, bf16[32,2,144,128]{3,2,1,0:T(8,128)(2,1)}, u32[]{:S(2)}, u32[]{:S(2)}) collective-permute-start(bf16[32,2,144,128]{3,2,1,0:T(8,128)(2,1)S(1)} %bitcast.92), channel_id=1, source_target_pairs={{1,0},{2,1},{3,2},{4,3},{5,4},{6,5},{7,6},{8,7},{9,8},{10,9},{11,1... | collective-permute-start | bytes 7077896 | tf_op jit(solution)/shard_map/ppermute | solution.py:20
  55.3 18.6 %copy-start.5 = (s32[16,4]{0,1:T(4,128)S(1)}, s32[16,4]{0,1:T(4,128)}, u32[]{:S(2)}) copy-start(s32[16,4]{0,1:T(4,128)} %param.15) | copy-start | bytes 772
  320.2 2.7 copy-start.1
